TPU v7x, 32 devices: a whole 2x2x4 slice. The times are simulated.
32 devices in a mesh: gx: 16 (over z, y, x), gy: 2 (over core).
Axes of the slice: x: 2, y: 2, z: 4, core: 2. Of those that a mesh axis runs over, the one named last changes fastest.
Arguments:
- node_latents: bfloat16 [16, 2, 256, 512], P('gx', 'gy'), may hold values from -6 to 6
- edge_latents: bfloat16 [16, 2, 768, 512], P('gx', 'gy'), may hold values from -6 to 6
- edge_w1: bfloat16 [1536, 512], replicated, may hold values from -0.15625 to 0.15625
- edge_b1: float32 [512], replicated, may hold values from -3 to 3
- edge_w2: bfloat16 [512, 512], replicated, may hold values from -0.25 to 0.25
- node_w1: bfloat16 [1024, 512], replicated, may hold values from -0.1875 to 0.1875
- node_b1: float32 [512], replicated, may hold values from -3 to 3
- node_w2: bfloat16 [512, 512], replicated, may hold values from -0.25 to 0.25
- node_cot: bfloat16 [16, 2, 256, 512], P('gx', 'gy'), may hold values from -6 to 6
- edge_cot: bfloat16 [16, 2, 768, 512], P('gx', 'gy'), may hold values from -6 to 6
- send_count: int32 [16, 2, 4], P('gx', 'gy'), may hold values from 0 to 2, as said below
- send_list: int32 [16, 2, 4, 2], P('gx', 'gy'), may hold values from 0 to 1
- tile_recv: int32 [16, 2, 6], P('gx', 'gy'), may hold values from 0 to 1
- tile_send: int32 [16, 2, 6], P('gx', 'gy'), may hold values from 0 to 9, as said below
- tile_perm: int32 [16, 2, 6, 128], P('gx', 'gy'), may hold values from 0 to 127, each once within a row
Outputs:
- node_out: bfloat16 [16, 2, 256, 512], P('gx', 'gy')
- node_grad: bfloat16 [16, 2, 256, 512], P('gx', 'gy')
- edge_grad: bfloat16 [16, 2, 768, 512], P('gx', 'gy')
- weight_dir: bfloat16 [1835008], P(('gx', 'gy'))
Inputs may be any that keep to these rules, and one draw needn't show every extreme that they name: `send_count`: entries for a neighbour outside the grid of partitions are 0, all others at least 1; the partition at (0, 0) sends 2 blocks to its neighbour at gx+1. `tile_send`: A value of 2 or more is a halo slot 2 + d * 2 + s that direction d's neighbour fills (s below its send count).
All inputs are finite; a program needn't handle non-finite values.
Results may differ from a plain program's by a relative error of at most 0.0075.
Values may be sent and summed in bfloat16 or wider, within the bound.
No kernel may reach another device: no remote copies, remote signals or barrier semaphores. Data moves between devices by JAX's collectives and lax.ppermute only.
A program may use at most 128 MiB of HBM per device.

v0:
```python
import jax
import jax.numpy as jnp
from jax import lax
from jax.sharding import PartitionSpec as P


def padded(block, sides, width):
    for axis, dim in sides:
        count = lax.axis_size(axis)
        forward = [(i, i + 1) for i in range(count - 1)]
        backward = [(target, source) for source, target in forward]
        low = lax.ppermute(
            lax.slice_in_dim(block, block.shape[dim] - width, None, axis=dim), axis, forward
        )
        high = lax.ppermute(lax.slice_in_dim(block, 0, width, axis=dim), axis, backward)
        block = jnp.concatenate([low, block, high], axis=dim)
    return block


def silu_slope(values):
    logistic = jax.nn.sigmoid(values)
    return logistic * (1.0 + values * (1.0 - logistic))


def layer_norm(values):
    center = values - jnp.mean(values, axis=-1, keepdims=True)
    inverse_rms = lax.rsqrt(jnp.mean(center * center, axis=-1, keepdims=True) + 1e-05)
    return (center * inverse_rms, inverse_rms)


def norm_back(normed, inverse_rms, upstream):
    return inverse_rms * (
        upstream
        - jnp.mean(upstream, axis=-1, keepdims=True)
        - normed * jnp.mean(upstream * normed, axis=-1, keepdims=True)
    )


def inner_rows(factor, second):
    return lax.dot_general(
        factor, second, (((0,), (0,)), ((), ())), preferred_element_type=jnp.float32
    )


def times_transposed(factor, second):
    return lax.dot_general(
        factor, second, (((1,), (1,)), ((), ())), preferred_element_type=jnp.float32
    )


def matmul(factor, second):
    return jnp.dot(factor, second, preferred_element_type=jnp.float32)


def fetch_halo(packed):
    row_halo = padded(jnp.stack([packed[1], packed[0]]), (("gx", 0),), 1)
    col_halo = padded(jnp.stack([packed[3], packed[2]]), (("gy", 0),), 1)
    return jnp.concatenate([row_halo[0], row_halo[3], col_halo[0], col_halo[3]], axis=0)


def return_partials(halo_part):
    row_back = padded(
        jnp.stack([halo_part[0], halo_part[1]]).astype(jnp.bfloat16), (("gx", 0),), 1
    ).astype(jnp.float32)
    col_back = padded(
        jnp.stack([halo_part[2], halo_part[3]]).astype(jnp.bfloat16), (("gy", 0),), 1
    ).astype(jnp.float32)
    return jnp.stack([row_back[3], row_back[0], col_back[3], col_back[0]])


def on_device(
    node_latents,
    edge_latents,
    edge_w1,
    edge_b1,
    edge_w2,
    node_w1,
    node_b1,
    node_w2,
    node_cot,
    edge_cot,
    send_count,
    send_list,
    tile_recv,
    tile_send,
    tile_perm,
):
    feature = node_latents.shape[3]
    block_size = tile_perm.shape[3]
    tile_count = tile_perm.shape[2]
    slot_count = send_list.shape[3]
    node_count = node_latents.shape[2]
    block_count = node_count // block_size
    node_blocks = node_latents.reshape(block_count, block_size, feature)
    local_rows = node_latents.reshape(node_count, feature)
    edge_rows = edge_latents.reshape(tile_count * block_size, feature)
    cot_node = node_cot.reshape(node_count, feature)
    cot_edge = edge_cot.reshape(tile_count * block_size, feature)
    send_counts = send_count.reshape(4)
    send_lists = send_list.reshape(4, slot_count)
    recv_idx = tile_recv.reshape(tile_count)
    send_idx = tile_send.reshape(tile_count)
    perm_idx = tile_perm.reshape(tile_count, block_size)
    live_slots = jnp.arange(slot_count, dtype=jnp.int32)[None, :] < send_counts[:, None]
    packed = jnp.where(
        live_slots[:, :, None, None], node_blocks[send_lists], jnp.zeros((), jnp.bfloat16)
    )
    offsets = jnp.arange(block_size, dtype=jnp.int32)
    recv_rows = (recv_idx[:, None] * block_size + offsets[None, :]).reshape(-1)
    send_rows = (send_idx[:, None] * block_size + perm_idx).reshape(-1)
    h_recv = local_rows[recv_rows]
    halo_blocks = fetch_halo(packed)
    flat_ext = jnp.concatenate([node_blocks, halo_blocks], axis=0).reshape(-1, feature)
    h_send = flat_ext[send_rows]
    joined = jnp.concatenate([edge_rows, h_recv, h_send], axis=1)
    edge_affine = matmul(joined, edge_w1) + edge_b1
    edge_hidden = jax.nn.silu(edge_affine).astype(jnp.bfloat16)
    edge_linear = matmul(edge_hidden, edge_w2)
    message, edge_inv = layer_norm(edge_linear)
    recv_hot = (recv_idx[None, :] == jnp.arange(block_count, dtype=jnp.int32)[:, None]).astype(
        jnp.float32
    )
    aggregate = jnp.einsum(
        "bt,tnf->bnf",
        recv_hot,
        message.reshape(tile_count, block_size, feature),
        precision=lax.Precision.HIGHEST,
    )
    aggregate = aggregate.reshape(node_count, feature).astype(jnp.bfloat16)
    node_input = jnp.concatenate([local_rows, aggregate], axis=1)
    node_affine = matmul(node_input, node_w1) + node_b1
    node_hidden = jax.nn.silu(node_affine).astype(jnp.bfloat16)
    node_linear = matmul(node_hidden, node_w2)
    node_normed, node_inv = layer_norm(node_linear)
    node_out = (local_rows.astype(jnp.float32) + node_normed).astype(jnp.bfloat16)
    grad_node_linear = norm_back(node_normed, node_inv, cot_node.astype(jnp.float32)).astype(
        jnp.bfloat16
    )
    g_nw2 = inner_rows(node_hidden, grad_node_linear)
    grad_node_affine = (
        times_transposed(grad_node_linear, node_w2) * silu_slope(node_affine)
    ).astype(jnp.bfloat16)
    g_nw1 = inner_rows(node_input, grad_node_affine)
    grad_node_input = times_transposed(grad_node_affine, node_w1)
    grad_direct = grad_node_input[:, :feature]
    grad_aggregate = grad_node_input[:, feature:]
    grad_message = grad_aggregate[recv_rows] + cot_edge.astype(jnp.float32)
    grad_edge_linear = norm_back(message, edge_inv, grad_message).astype(jnp.bfloat16)
    g_ew2 = inner_rows(edge_hidden, grad_edge_linear)
    grad_edge_affine = (
        times_transposed(grad_edge_linear, edge_w2) * silu_slope(edge_affine)
    ).astype(jnp.bfloat16)
    g_ew1 = inner_rows(joined, grad_edge_affine)
    grad_joined = times_transposed(grad_edge_affine, edge_w1)
    grad_e = grad_joined[:, :feature]
    grad_r = grad_joined[:, feature : 2 * feature]
    grad_s = grad_joined[:, 2 * feature :]
    edge_grad = (cot_edge.astype(jnp.float32) + grad_e).astype(jnp.bfloat16)
    grad_recv = jnp.einsum(
        "bt,tnf->bnf",
        recv_hot,
        grad_r.reshape(tile_count, block_size, feature),
        precision=lax.Precision.HIGHEST,
    )
    inverse = jnp.argsort(perm_idx, axis=1)
    grad_send = jnp.take_along_axis(
        grad_s.reshape(tile_count, block_size, feature), inverse[:, :, None], axis=1
    )
    extended_count = block_count + 4 * slot_count
    send_hot = (send_idx[None, :] == jnp.arange(extended_count, dtype=jnp.int32)[:, None]).astype(
        jnp.float32
    )
    partial_sum = jnp.einsum("bt,tnf->bnf", send_hot, grad_send, precision=lax.Precision.HIGHEST)
    owned_part = (
        partial_sum[:block_count]
        + grad_recv
        + grad_direct.reshape(block_count, block_size, feature)
    )
    halo_part = partial_sum[block_count:].reshape(4, slot_count, block_size, feature)
    returned = return_partials(halo_part)
    back_hot = (
        (send_lists[:, :, None] == jnp.arange(block_count, dtype=jnp.int32)[None, None, :])
        & live_slots[:, :, None]
    ).astype(jnp.float32)
    contrib = jnp.einsum("qsb,qsnf->bnf", back_hot, returned, precision=lax.Precision.HIGHEST)
    node_grad = (
        cot_node.reshape(block_count, block_size, feature).astype(jnp.float32)
        + owned_part
        + contrib
    )
    node_grad = node_grad.astype(jnp.bfloat16).reshape(1, 1, node_count, feature)
    weight_grad = jnp.concatenate([g_ew1, g_ew2, g_nw1, g_nw2], axis=0)
    total_entries = 7 * feature * feature
    share_len = total_entries // lax.axis_size(("gx", "gy"))
    summed = lax.psum(weight_grad, ("gx", "gy"))
    bounds = [0, 3 * feature, 4 * feature, 6 * feature, 7 * feature]
    pieces = []
    for index in range(4):
        matrix = summed[bounds[index] : bounds[index + 1]]
        pieces.append(matrix * lax.rsqrt(jnp.mean(matrix * matrix) + 1e-06))
    normalized = jnp.concatenate(pieces, axis=0).reshape(total_entries)
    own_start = lax.axis_index(("gx", "gy")) * share_len
    weight_dir = lax.dynamic_slice_in_dim(normalized, own_start, share_len).astype(jnp.bfloat16)
    return (
        node_out.reshape(1, 1, node_count, feature),
        node_grad,
        edge_grad.reshape(1, 1, tile_count * block_size, feature),
        weight_dir,
    )


def solution(mesh):
    placed = (
        P("gx", "gy", None, None),
        P("gx", "gy", None, None),
        P(),
        P(),
        P(),
        P(),
        P(),
        P(),
        P("gx", "gy", None, None),
        P("gx", "gy", None, None),
        P("gx", "gy", None),
        P("gx", "gy", None, None),
        P("gx", "gy", None),
        P("gx", "gy", None),
        P("gx", "gy", None, None),
    )
    return jax.shard_map(
        on_device,
        mesh=mesh,
        in_specs=placed,
        out_specs=(
            P("gx", "gy", None, None),
            P("gx", "gy", None, None),
            P("gx", "gy", None, None),
            P(("gx", "gy")),
        ),
        check_vma=False,
    )
```

profile of v0, /device:TPU:0, one launch (start us, length us, event | category | flops | bytes accessed | tf_op | source)
XLA Modules:
  0.0 270.5 jit_solution(10264045444098275007)
XLA Ops:
  9.8 1.6 gather_fusion.1
  12.6 5.6 %collective-permute-start = (bf16[1,2,128,512]{3,2,1,0:T(8,128)(2,1)}, bf16[1,2,128,512]{3,2,1,0:T(8,128)(2,1)}, u32[]{:S(2)}, u32[]{:S(2)}) collective-permute-start(bf16[1,2,128,512]{3,2,1,0:T(8,128)(2,1)} %get-tuple-element.28), channel_id=1, source_target_pairs={{0,2},{2,4},{4,6},{6,8},{8,10},{10,12},{12,14},{14,16},{16,18},{18... | collective-permute-start | bytes 786440 | tf_op jit(solution)/shard_map/ppermute | solution.py:12
  19.4 2.2 collective-permute-start.2
  24.5 3.4 %gather_fusion = bf16[768,512]{1,0:T(8,128)(2,1)} fusion(bf16[256,512]{1,0:T(8,128)(2,1)S(1)} %bitcast.130, s32[1024]{0:T(1024)S(1)} %get-tuple-element.40), kind=kCustom, calls=%fused_computation | custom fusion | bytes 1575936 | tf_op jit(solution)/shard_map/gather | solution.py:111
  33.8 3.3 %gather_fusion.2 = bf16[768,512]{1,0:T(8,128)(2,1)} fusion(bf16[1280,512]{1,0:T(8,128)(2,1)S(1)} %bitcast.134, s32[1024]{0:T(1024)S(1)} %get-tuple-element.39), kind=kCustom, calls=%fused_computation.2 | custom fusion | bytes 1575936 | tf_op jit(solution)/shard_map/gather | solution.py:114
  37.1 4.3 %multiply_convert_fusion.2 = (bf16[768,512]{1,0:T(8,128)(2,1)S(1)}, f32[768,512]{1,0:T(8,128)}) fusion(f32[512]{0:T(512)S(1)} %copy-done.26, bf16[1536,512]{1,0:T(8,128)(2,1)S(1)} %copy-done, bf16[768,512]{1,0:T(8,128)(2,1)} %gather_fusion.2, bf16[768,512]{1,0:T(8,128)(2,1)} %gather_fusion, bf16[768,512]{1,0:T(8,128)(2,1)} %bitcast.150), kind=kOutput, calls=%fused_computation.28 | convolution fusion | flops 1217396736 | bytes 6293504 | tf_op jit(solution)/shard_map/dot_general | solution.py:52
  43.3 1.9 fusion.12
  47.8 1.5 fusion.54
  50.3 1.8 fusion.29
  53.0 3.2 %gather_fusion.3 = f32[768,512]{1,0:T(8,128)} fusion(f32[256,512]{1,0:T(8,128)S(1)} %get-tuple-element.23, s32[1024]{0:T(1024)S(1)} %get-tuple-element.40), kind=kCustom, calls=%fused_computation.3 | custom fusion | bytes 3148800 | tf_op jit(solution)/shard_map/gather | solution.py:147
  56.1 2.7 fusion.20
  63.3 1.4 fusion.17
  65.1 3.4 %pad_maximum_fusion = f32[3584,512]{1,0:T(8,128)} fusion(f32[512,512]{1,0:T(8,128)S(1)} %copy-done.13, f32[1024,512]{1,0:T(8,128)S(1)} %copy-done.6, f32[512,512]{1,0:T(8,128)S(1)} %fusion.65, f32[1536,512]{1,0:T(8,128)S(1)} %fusion.17), kind=kLoop, calls=%fused_computation.5 | loop fusion | flops 5505024 | bytes 14680064 | tf_op jit(solution)/shard_map/concatenate | solution.py:192
  70.1 1.4 fusion.64
  71.5 1.9 fusion.19
  73.4 7.8 %gather_fusion.4 = f32[768,512]{1,0:T(8,128)} fusion(f32[6,128,512]{2,1,0:T(8,128)S(1)} %bitcast.133, s32[768]{0:T(1024)S(1)} %fusion.33), kind=kCustom, calls=%fused_computation.4 | custom fusion | bytes 3151872 | tf_op jit(solution)/shard_map/jit(take_along_axis)/gather | solution.py:166
  81.2 4.7 %fusion.62 = (bf16[10,128,512]{2,0,1:T(8,128)(2,1)S(1)}, f32[10,128,512]{2,0,1:T(8,128)S(1)}) fusion(f32[6,128,512]{2,1,0:T(8,128)} %bitcast.137, pred[6,128]{0,1:T(8,128)(4,1)S(1)} %copy.42, s32[6]{0:T(128)S(1)} %bitcast.149), kind=kOutput, calls=%fused_computation.139 | convolution fusion | flops 48234556 | bytes 5505816 | tf_op jit(solution)/shard_map/bt,tnf->bnf/dot_general | solution.py:173
  86.8 3.4 %collective-permute-start.4 = (bf16[1,2,128,512]{3,1,2,0:T(2,128)(2,1)S(1)}, bf16[1,2,128,512]{3,1,2,0:T(2,128)(2,1)S(1)}, u32[]{:S(2)}, u32[]{:S(2)}) collective-permute-start(bf16[1,2,128,512]{3,1,2,0:T(2,128)(2,1)S(1)} %get-tuple-element.15), channel_id=1, source_target_pairs={{0,2},{2,4},{4,6},{6,8},{8,10},{10,12},{12,14},{14,16},{16,18},{18... | collective-permute-start | bytes 786440 | tf_op jit(solution)/shard_map/ppermute | solution.py:12
  91.6 2.5 collective-permute-start.6
  94.1 1.5 collective-permute-start.7
  95.6 1.9 fusion.2
  97.7 6.4 %collective-permute-done.4 = bf16[1,2,128,512]{3,1,2,0:T(2,128)(2,1)S(1)} collective-permute-done((bf16[1,2,128,512]{3,1,2,0:T(2,128)(2,1)S(1)}, bf16[1,2,128,512]{3,1,2,0:T(2,128)(2,1)S(1)}, u32[]{:S(2)}, u32[]{:S(2)}) %collective-permute-start.4) | collective-permute-done | bytes 262176 | tf_op jit(solution)/shard_map/ppermute | solution.py:12
  104.1 3.6 %collective-permute-done.5 = bf16[1,2,128,512]{3,1,2,0:T(2,128)(2,1)S(1)} collective-permute-done((bf16[1,2,128,512]{3,1,2,0:T(2,128)(2,1)S(1)}, bf16[1,2,128,512]{3,1,2,0:T(2,128)(2,1)S(1)}, u32[]{:S(2)}, u32[]{:S(2)}) %collective-permute-start.5) | collective-permute-done | bytes 262176 | tf_op jit(solution)/shard_map/ppermute | solution.py:15
  110.2 3.2 %fusion.8 = f32[2,128,512]{2,0,1:T(2,128)S(1)} fusion(f32[4,2,128,512]{3,1,2,0:T(2,128)S(1)} %pad_maximum_fusion.2, pred[4,2]{0,1:T(4,128)(4,1)S(1)} %iota_compare_fusion.1, s32[4,2]{0,1:T(2,128)S(1)} %bitcast.146), kind=kOutput, calls=%fused_computation.32 | convolution fusion | flops 12582944 | bytes 2621480 | tf_op jit(solution)/shard_map/qsb,qsnf->bnf/dot_general | solution.py:185
  114.4 128.1 %all-reduce.2.cloned.1.call-done = f32[3584,512]{1,0:T(8,128)} async-done(((f32[3584,512]{1,0:T(8,128)}), f32[3584,512]{1,0:T(8,128)}) %all-reduce.2.cloned.1.call-update) | async-done | bytes 7340048 | tf_op jit(solution)/shard_map/psum | solution.py:195
  242.5 3.3 %multiply_reduce_fusion = f32[]{:T(128)} fusion(f32[3584,512]{1,0:T(8,128)} %all-reduce.2.cloned.1.call-done), kind=kLoop, calls=%fused_computation.7 | loop fusion | flops 1572863 | bytes 3145732 | tf_op jit(solution)/shard_map/reduce_sum | solution.py:200
  246.5 2.7 %multiply_reduce_fusion.1 = f32[]{:T(128)} fusion(f32[3584,512]{1,0:T(8,128)} %all-reduce.2.cloned.1.call-done), kind=kLoop, calls=%fused_computation.19 | loop fusion | flops 1048575 | bytes 2097156 | tf_op jit(solution)/shard_map/reduce_sum | solution.py:200
  249.9 2.5 multiply_reduce_fusion.5
  253.8 2.3 slice_multiply_fusion
  256.1 1.9 slice_multiply_fusion.1
  258.0 1.8 slice_multiply_fusion.3
  260.5 1.9 copy.54
  (126 shorter events, 32.4 us)
Async XLA Ops:
  8.0 29.1 %copy-start = (bf16[1536,512]{1,0:T(8,128)(2,1)S(1)}, bf16[1536,512]{1,0:T(8,128)(2,1)}, u32[]{:S(2)}) copy-start(bf16[1536,512]{1,0:T(8,128)(2,1)} %param.17) | copy-start | bytes 4718596
  8.0 60.5 %sort.19.cloned.1.call-start = ((), (), s32[]{:S(2)}) async-start(), calls=%async_computation.1 | async-start | bytes 24608 | tf_op jit(solution)/shard_map/jit(argsort)/sort | solution.py:165
  11.5 11.3 %copy-start.19 = (s32[1,1,6,128]{3,1,2,0:T(1,128)S(1)}, s32[1,1,6,128]{3,1,2,0:T(1,128)}, u32[]{:S(2)}) copy-start(s32[1,1,6,128]{3,1,2,0:T(1,128)} %param.29) | copy-start | bytes 9220
  11.5 12.6 %copy-start.21 = (s32[1,1,6]{2,1,0:T(1,128)S(1)}, s32[1,1,6]{2,1,0:T(1,128)}, u32[]{:S(2)}) copy-start(s32[1,1,6]{2,1,0:T(1,128)} %param.27) | copy-start | bytes 76
  11.6 12.7 %copy-start.22 = (s32[1,1,6]{2,1,0:T(1,128)S(1)}, s32[1,1,6]{2,1,0:T(1,128)}, u32[]{:S(2)}) copy-start(s32[1,1,6]{2,1,0:T(1,128)} %param.28) | copy-start | bytes 76
  11.6 12.8 %copy-start.11 = (bf16[1,1,256,512]{3,2,1,0:T(8,128)(2,1)S(1)}, bf16[1,1,256,512]{3,2,1,0:T(8,128)(2,1)}, u32[]{:S(2)}) copy-start(bf16[1,1,256,512]{3,2,1,0:T(8,128)(2,1)} %param.23) | copy-start | bytes 786436
  11.6 12.9 %copy-start.1 = (bf16[1,1,256,512]{3,2,1,0:T(8,128)(2,1)S(1)}, bf16[1,1,256,512]{3,2,1,0:T(8,128)(2,1)}, u32[]{:S(2)}) copy-start(bf16[1,1,256,512]{3,2,1,0:T(8,128)(2,1)} %param.15) | copy-start | bytes 786436
  12.6 16.4 %collective-permute-start = (bf16[1,2,128,512]{3,2,1,0:T(8,128)(2,1)}, bf16[1,2,128,512]{3,2,1,0:T(8,128)(2,1)}, u32[]{:S(2)}, u32[]{:S(2)}) collective-permute-start(bf16[1,2,128,512]{3,2,1,0:T(8,128)(2,1)} %get-tuple-element.28), channel_id=1, source_target_pairs={{0,2},{2,4},{4,6},{6,8},{8,10},{10,12},{12,14},{14,16},{16,18},{18... | collective-permute-start | bytes 786440 | tf_op jit(solution)/shard_map/ppermute | solution.py:12
  18.1 12.7 %collective-permute-start.1 = (bf16[1,2,128,512]{3,2,1,0:T(8,128)(2,1)}, bf16[1,2,128,512]{3,2,1,0:T(8,128)(2,1)}, u32[]{:S(2)}, u32[]{:S(2)}) collective-permute-start(bf16[1,2,128,512]{3,2,1,0:T(8,128)(2,1)} %get-tuple-element.27), channel_id=1, source_target_pairs={{2,0},{4,2},{6,4},{8,6},{10,8},{12,10},{14,12},{16,14},{18,16},{20... | collective-permute-start | bytes 786440 | tf_op jit(solution)/shard_map/ppermute | solution.py:15
  19.4 12.4 %collective-permute-start.2 = (bf16[1,2,128,512]{3,2,1,0:T(8,128)(2,1)}, bf16[1,2,128,512]{3,2,1,0:T(8,128)(2,1)}, u32[]{:S(2)}, u32[]{:S(2)}) collective-permute-start(bf16[1,2,128,512]{3,2,1,0:T(8,128)(2,1)} %get-tuple-element.26), channel_id=1, source_target_pairs={{0,1},{2,3},{4,5},{6,7},{8,9},{10,11},{12,13},{14,15},{16,17},{18,... | collective-permute-start | bytes 786440 | tf_op jit(solution)/shard_map/ppermute | solution.py:12
  21.6 11.2 %collective-permute-start.3 = (bf16[1,2,128,512]{3,2,1,0:T(8,128)(2,1)}, bf16[1,2,128,512]{3,2,1,0:T(8,128)(2,1)}, u32[]{:S(2)}, u32[]{:S(2)}) collective-permute-start(bf16[1,2,128,512]{3,2,1,0:T(8,128)(2,1)} %get-tuple-element.25), channel_id=1, source_target_pairs={{1,0},{3,2},{5,4},{7,6},{9,8},{11,10},{13,12},{15,14},{17,16},{19,... | collective-permute-start | bytes 786440 | tf_op jit(solution)/shard_map/ppermute | solution.py:15
  24.1 218.4 %all-reduce.2.cloned.1.call-start = ((), (), s32[]{:S(2)}) async-start(), calls=%async_computation | async-start | bytes 14680064 | tf_op jit(solution)/shard_map/psum | solution.py:195
  33.8 3.3 %copy-start.26 = (f32[512]{0:T(512)S(1)}, f32[512]{0:T(512)}, u32[]{:S(2)}) copy-start(f32[512]{0:T(512)} %param.18) | copy-start | bytes 6148
  37.1 4.3 %copy-start.17 = (bf16[512,512]{1,0:T(8,128)(2,1)S(1)}, bf16[512,512]{1,0:T(8,128)(2,1)}, u32[]{:S(2)}) copy-start(bf16[512,512]{1,0:T(8,128)(2,1)} %param.19) | copy-start | bytes 1572868
  43.3 2.0 copy-start.14
  43.3 2.0 copy-start.25
  53.0 3.2 %copy-start.7 = (bf16[1,1,768,512]{3,2,1,0:T(8,128)(2,1)S(1)}, bf16[1,1,768,512]{3,2,1,0:T(8,128)(2,1)}, u32[]{:S(2)}) copy-start(bf16[1,1,768,512]{3,2,1,0:T(8,128)(2,1)} %param.24) | copy-start | bytes 2359300
  56.1 2.7 %copy-start.3 = (f32[768,512]{1,0:T(8,128)S(1)}, f32[768,512]{1,0:T(8,128)}, u32[]{:S(2)}) copy-start(f32[768,512]{1,0:T(8,128)} %copy-done.2) | copy-start | bytes 4718596
  56.1 2.8 %copy-start.4 = (f32[768,512]{1,0:T(8,128)S(1)}, f32[768,512]{1,0:T(8,128)}, u32[]{:S(2)}) copy-start(f32[768,512]{1,0:T(8,128)} %gather_fusion.3) | copy-start | bytes 4718596
  60.1 1.6 copy-start.27
  61.7 1.4 copy-start.16
  61.7 1.6 copy-start.23
  63.3 1.6 copy-start.6
  63.3 1.9 copy-start.13
  70.1 1.4 copy-start.8
  86.0 9.6 %copy-start.5 = (f32[768,512]{1,0:T(8,128)S(1)}, f32[768,512]{1,0:T(8,128)}, u32[]{:S(2)}) copy-start(f32[768,512]{1,0:T(8,128)} %get-tuple-element.13) | copy-start | bytes 4718596
  86.8 17.3 %collective-permute-start.4 = (bf16[1,2,128,512]{3,1,2,0:T(2,128)(2,1)S(1)}, bf16[1,2,128,512]{3,1,2,0:T(2,128)(2,1)S(1)}, u32[]{:S(2)}, u32[]{:S(2)}) collective-permute-start(bf16[1,2,128,512]{3,1,2,0:T(2,128)(2,1)S(1)} %get-tuple-element.15), channel_id=1, source_target_pairs={{0,2},{2,4},{4,6},{6,8},{8,10},{10,12},{12,14},{14,16},{16,18},{18... | collective-permute-start | bytes 786440 | tf_op jit(solution)/shard_map/ppermute | solution.py:12
  90.3 17.5 %collective-permute-start.5 = (bf16[1,2,128,512]{3,1,2,0:T(2,128)(2,1)S(1)}, bf16[1,2,128,512]{3,1,2,0:T(2,128)(2,1)S(1)}, u32[]{:S(2)}, u32[]{:S(2)}) collective-permute-start(bf16[1,2,128,512]{3,1,2,0:T(2,128)(2,1)S(1)} %get-tuple-element.18), channel_id=1, source_target_pairs={{2,0},{4,2},{6,4},{8,6},{10,8},{12,10},{14,12},{16,14},{18,16},{20... | collective-permute-start | bytes 786440 | tf_op jit(solution)/shard_map/ppermute | solution.py:15
  91.6 16.8 %collective-permute-start.6 = (bf16[1,2,128,512]{3,1,2,0:T(2,128)(2,1)S(1)}, bf16[1,2,128,512]{3,1,2,0:T(2,128)(2,1)S(1)}, u32[]{:S(2)}, u32[]{:S(2)}) collective-permute-start(bf16[1,2,128,512]{3,1,2,0:T(2,128)(2,1)S(1)} %get-tuple-element.17), channel_id=1, source_target_pairs={{0,1},{2,3},{4,5},{6,7},{8,9},{10,11},{12,13},{14,15},{16,17},{18,... | collective-permute-start | bytes 786440 | tf_op jit(solution)/shard_map/ppermute | solution.py:12
  94.1 14.3 %collective-permute-start.7 = (bf16[1,2,128,512]{3,1,2,0:T(2,128)(2,1)S(1)}, bf16[1,2,128,512]{3,1,2,0:T(2,128)(2,1)S(1)}, u32[]{:S(2)}, u32[]{:S(2)}) collective-permute-start(bf16[1,2,128,512]{3,1,2,0:T(2,128)(2,1)S(1)} %get-tuple-element.16), channel_id=1, source_target_pairs={{1,0},{3,2},{5,4},{7,6},{9,8},{11,10},{13,12},{15,14},{17,16},{19,... | collective-permute-start | bytes 786440 | tf_op jit(solution)/shard_map/ppermute | solution.py:15
  109.0 1.2 copy-start.20
  110.1 3.3 %copy-start.12 = (f32[256,512]{1,0:T(8,128)S(1)}, f32[256,512]{1,0:T(8,128)}, u32[]{:S(2)}) copy-start(f32[256,512]{1,0:T(8,128)} %get-tuple-element.24) | copy-start | bytes 1572868
  (6 other events, 6.5 us)
Sparse Core Ops, SparseCore 0:
  24.2 2.3 sort.21.cloned.1.call-done
  (1 shorter events, 0.0 us)
Sparse Core Ops, SparseCore 1:
  68.6 173.8 all-reduce.1
where the time goes:
time: 271 us
  waiting for transfers between devices  140 us (52%)
  local copies, waits for them, and re-layouts  34.2 us (13%)
  other arithmetic  32 us (12%)
  matrix products  26.2 us (10%)
  starting transfers between devices  19.1 us (7%)
  between operations  18.9 us (7%)
    psum x1, waiting for transfers between devices, on_device(): summed = lax.psum(weight_grad, ('gx', 'gy'))  128 us
    ppermute x4, starting transfers between devices, padded(): lax.ppermute(lax.slice_in_dim(block, block.shape[dim] - width, None, axis...  13.7 us
    unnamed x64, local copies, waits for them, and re-layouts  9.38 us
    reduce_sum x3, other arithmetic, on_device(): pieces.append(matrix * lax.rsqrt(jnp.mean(matrix * matrix) + 1e-06))  8.52 us
    gather x1, local copies, waits for them, and re-layouts, on_device(): jnp.take_along_axis(grad_s.reshape(tile_count, block_size, feature), inve...  7.83 us
    ppermute x4, waiting for transfers between devices, padded(): lax.ppermute(lax.slice_in_dim(block, block.shape[dim] - width, None, axis...  7.47 us
    mul x3, other arithmetic, on_device(): pieces.append(matrix * lax.rsqrt(jnp.mean(matrix * matrix) + 1e-06))  5.99 us
    dot_general x4, matrix products, matmul(): return jnp.dot(factor, second, preferred_element_type=jnp.float32)  5.82 us
  transfers between devices with their start and end apart: 9, of which 5 were waited for; matrix products, arithmetic and copies ran while one was open for 13% of the time, Pallas kernels for 0%

commit v1 on v0

--- a/solution.py
+++ b/solution.py
@@ -192,7 +192,9 @@
     weight_grad = jnp.concatenate([g_ew1, g_ew2, g_nw1, g_nw2], axis=0)
     total_entries = 7 * feature * feature
     share_len = total_entries // lax.axis_size(("gx", "gy"))
-    summed = lax.psum(weight_grad, ("gx", "gy"))
+    summed = weight_grad
+    for over in ("gy", "gx"):
+        summed = lax.psum(summed, over)
     bounds = [0, 3 * feature, 4 * feature, 6 * feature, 7 * feature]
     pieces = []
     for index in range(4):

time: 271 us -> 377 us (1.39)
  waiting for transfers between devices: 140 us -> 246 us
    psum x1 -> x2, waiting for transfers between devices: 128 us -> 236 us  [on_device(): summed = lax.psum(summed, over)]
    ppermute x4, waiting for transfers between devices: 7.47 us -> 2.31 us  [padded(): lax.ppermute(lax.slice_in_dim(block, block.shape[dim] - width, None, axis...]
  transfers between devices with their start and end apart: 9 -> 10, of which waited for: 5 -> 5; matrix products, arithmetic and copies ran while one was open for 13% -> 9% of each run, Pallas kernels for 0% -> 0%
where the time goes in v1:
time: 377 us; the launch traced here: 376 us
  waiting for transfers between devices  246 us (65%)
  local copies, waits for them, and re-layouts  34.2 us (9%)
  other arithmetic  32 us (8%)
  matrix products  26.4 us (7%)
  starting transfers between devices  18.8 us (5%)
  between operations  18.8 us (5%)
    psum x2, waiting for transfers between devices, on_device(): summed = lax.psum(summed, over)  236 us
    ppermute x4, starting transfers between devices, padded(): lax.ppermute(lax.slice_in_dim(block, block.shape[dim] - width, None, axis...  13.3 us
    unnamed x64, local copies, waits for them, and re-layouts  9.38 us
    reduce_sum x3, other arithmetic, on_device(): pieces.append(matrix * lax.rsqrt(jnp.mean(matrix * matrix) + 1e-06))  8.51 us
    gather x1, local copies, waits for them, and re-layouts, on_device(): jnp.take_along_axis(grad_s.reshape(tile_count, block_size, feature), inve...  7.83 us
    ppermute x4, waiting for transfers between devices, padded(): lax.ppermute(lax.slice_in_dim(block, 0, width, axis=dim), axis, backward)  7.73 us
  transfers between devices with their start and end apart: 10, of which 5 were waited for; matrix products, arithmetic and copies ran while one was open for 9% of the time, Pallas kernels for 0%

profile of v1, /device:TPU:0, one launch (start us, length us, event | category | flops | bytes accessed | tf_op | source)
XLA Modules:
  0.0 376.5 jit_solution(8669624442300811124)
XLA Ops:
  9.8 1.6 gather_fusion.1
  12.6 5.6 %collective-permute-start = (bf16[1,2,128,512]{3,2,1,0:T(8,128)(2,1)}, bf16[1,2,128,512]{3,2,1,0:T(8,128)(2,1)}, u32[]{:S(2)}, u32[]{:S(2)}) collective-permute-start(bf16[1,2,128,512]{3,2,1,0:T(8,128)(2,1)} %get-tuple-element.28), channel_id=1, source_target_pairs={{0,2},{2,4},{4,6},{6,8},{8,10},{10,12},{12,14},{14,16},{16,18},{18... | collective-permute-start | bytes 786440 | tf_op jit(solution)/shard_map/ppermute | solution.py:12
  19.4 2.2 collective-permute-start.2
  23.3 3.4 gather_fusion
  26.6 2.3 collective-permute-done
  33.8 3.3 gather_fusion.2
  37.1 4.3 %multiply_convert_fusion.2 = (bf16[768,512]{1,0:T(8,128)(2,1)S(1)}, f32[768,512]{1,0:T(8,128)}) fusion(f32[512]{0:T(512)S(1)} %copy-done.26, bf16[1536,512]{1,0:T(8,128)(2,1)S(1)} %copy-done, bf16[768,512]{1,0:T(8,128)(2,1)} %gather_fusion.2, bf16[768,512]{1,0:T(8,128)(2,1)} %gather_fusion, bf16[768,512]{1,0:T(8,128)(2,1)} %bitcast.150), kind=kOutput, calls=%fused_computation.28 | convolution fusion | flops 1217396736 | bytes 6293504 | tf_op jit(solution)/shard_map/dot_general | solution.py:52
  43.3 1.9 fusion.12
  47.8 1.5 fusion.54
  50.3 1.8 fusion.29
  53.0 3.2 gather_fusion.3
  56.1 2.7 fusion.20
  63.3 1.4 fusion.17
  65.1 3.4 pad_maximum_fusion
  69.8 33.5 %all-reduce.3.cloned.1.call-done = f32[3584,512]{1,0:T(8,128)} async-done(((f32[3584,512]{1,0:T(8,128)}), f32[3584,512]{1,0:T(8,128)}) %all-reduce.3.cloned.1.call-update) | async-done | bytes 7340048 | tf_op jit(solution)/shard_map/psum | solution.py:197
  106.3 1.9 fusion.19
  108.2 7.8 %gather_fusion.4 = f32[768,512]{1,0:T(8,128)} fusion(f32[6,128,512]{2,1,0:T(8,128)S(1)} %bitcast.133, s32[768]{0:T(1024)S(1)} %fusion.33), kind=kCustom, calls=%fused_computation.4 | custom fusion | bytes 3151872 | tf_op jit(solution)/shard_map/jit(take_along_axis)/gather | solution.py:166
  116.1 4.9 %fusion.62 = (bf16[10,128,512]{2,0,1:T(8,128)(2,1)S(1)}, f32[10,128,512]{2,0,1:T(8,128)S(1)}) fusion(f32[6,128,512]{2,1,0:T(8,128)} %bitcast.137, pred[6,128]{0,1:T(8,128)(4,1)S(1)} %copy.42, s32[6]{0:T(128)S(1)} %bitcast.149), kind=kOutput, calls=%fused_computation.139 | convolution fusion | flops 48234556 | bytes 5505816 | tf_op jit(solution)/shard_map/bt,tnf->bnf/dot_general | solution.py:173
  121.8 3.7 collective-permute-start.4
  126.8 1.9 collective-permute-start.6
  128.7 1.5 collective-permute-start.7
  130.2 1.9 fusion.2
  132.3 6.8 %collective-permute-done.5 = bf16[1,2,128,512]{3,1,2,0:T(2,128)(2,1)S(1)} collective-permute-done((bf16[1,2,128,512]{3,1,2,0:T(2,128)(2,1)S(1)}, bf16[1,2,128,512]{3,1,2,0:T(2,128)(2,1)S(1)}, u32[]{:S(2)}, u32[]{:S(2)}) %collective-permute-start.5) | collective-permute-done | bytes 262176 | tf_op jit(solution)/shard_map/ppermute | solution.py:15
  141.5 3.2 fusion.8
  145.8 202.8 %all-reduce.5.cloned.1.call-done = f32[3584,512]{1,0:T(8,128)} async-done(((f32[3584,512]{1,0:T(8,128)}), f32[3584,512]{1,0:T(8,128)}) %all-reduce.5.cloned.1.call-update) | async-done | bytes 7340048 | tf_op jit(solution)/shard_map/psum | solution.py:197
  348.6 3.3 multiply_reduce_fusion
  352.6 2.7 multiply_reduce_fusion.1
  356.0 2.5 multiply_reduce_fusion.5
  359.8 2.3 slice_multiply_fusion
  362.1 1.9 slice_multiply_fusion.1
  364.0 1.8 slice_multiply_fusion.3
  366.5 1.9 copy.54
  (129 shorter events, 32.9 us)
Async XLA Ops:
  8.0 29.1 %copy-start = (bf16[1536,512]{1,0:T(8,128)(2,1)S(1)}, bf16[1536,512]{1,0:T(8,128)(2,1)}, u32[]{:S(2)}) copy-start(bf16[1536,512]{1,0:T(8,128)(2,1)} %param.17) | copy-start | bytes 4718596
  8.0 95.3 %all-reduce.3.cloned.1.call-start = ((), (), s32[]{:S(2)}) async-start(), calls=%async_computation | async-start | bytes 14680064 | tf_op jit(solution)/shard_map/psum | solution.py:197
  11.5 11.3 %copy-start.21 = (s32[1,1,6]{2,1,0:T(1,128)S(1)}, s32[1,1,6]{2,1,0:T(1,128)}, u32[]{:S(2)}) copy-start(s32[1,1,6]{2,1,0:T(1,128)} %param.27) | copy-start | bytes 76
  11.5 11.4 %copy-start.22 = (s32[1,1,6]{2,1,0:T(1,128)S(1)}, s32[1,1,6]{2,1,0:T(1,128)}, u32[]{:S(2)}) copy-start(s32[1,1,6]{2,1,0:T(1,128)} %param.28) | copy-start | bytes 76
  11.6 11.5 %copy-start.11 = (bf16[1,1,256,512]{3,2,1,0:T(8,128)(2,1)S(1)}, bf16[1,1,256,512]{3,2,1,0:T(8,128)(2,1)}, u32[]{:S(2)}) copy-start(bf16[1,1,256,512]{3,2,1,0:T(8,128)(2,1)} %param.23) | copy-start | bytes 786436
  11.6 11.6 %copy-start.19 = (s32[1,1,6,128]{3,1,2,0:T(1,128)S(1)}, s32[1,1,6,128]{3,1,2,0:T(1,128)}, u32[]{:S(2)}) copy-start(s32[1,1,6,128]{3,1,2,0:T(1,128)} %param.29) | copy-start | bytes 9220
  11.6 11.7 %copy-start.1 = (bf16[1,1,256,512]{3,2,1,0:T(8,128)(2,1)S(1)}, bf16[1,1,256,512]{3,2,1,0:T(8,128)(2,1)}, u32[]{:S(2)}) copy-start(bf16[1,1,256,512]{3,2,1,0:T(8,128)(2,1)} %param.15) | copy-start | bytes 786436
  12.6 16.4 %collective-permute-start = (bf16[1,2,128,512]{3,2,1,0:T(8,128)(2,1)}, bf16[1,2,128,512]{3,2,1,0:T(8,128)(2,1)}, u32[]{:S(2)}, u32[]{:S(2)}) collective-permute-start(bf16[1,2,128,512]{3,2,1,0:T(8,128)(2,1)} %get-tuple-element.28), channel_id=1, source_target_pairs={{0,2},{2,4},{4,6},{6,8},{8,10},{10,12},{12,14},{14,16},{16,18},{18... | collective-permute-start | bytes 786440 | tf_op jit(solution)/shard_map/ppermute | solution.py:12
  18.1 12.7 %collective-permute-start.1 = (bf16[1,2,128,512]{3,2,1,0:T(8,128)(2,1)}, bf16[1,2,128,512]{3,2,1,0:T(8,128)(2,1)}, u32[]{:S(2)}, u32[]{:S(2)}) collective-permute-start(bf16[1,2,128,512]{3,2,1,0:T(8,128)(2,1)} %get-tuple-element.27), channel_id=1, source_target_pairs={{2,0},{4,2},{6,4},{8,6},{10,8},{12,10},{14,12},{16,14},{18,16},{20... | collective-permute-start | bytes 786440 | tf_op jit(solution)/shard_map/ppermute | solution.py:15
  19.4 12.4 %collective-permute-start.2 = (bf16[1,2,128,512]{3,2,1,0:T(8,128)(2,1)}, bf16[1,2,128,512]{3,2,1,0:T(8,128)(2,1)}, u32[]{:S(2)}, u32[]{:S(2)}) collective-permute-start(bf16[1,2,128,512]{3,2,1,0:T(8,128)(2,1)} %get-tuple-element.26), channel_id=1, source_target_pairs={{0,1},{2,3},{4,5},{6,7},{8,9},{10,11},{12,13},{14,15},{16,17},{18,... | collective-permute-start | bytes 786440 | tf_op jit(solution)/shard_map/ppermute | solution.py:12
  21.6 11.2 %collective-permute-start.3 = (bf16[1,2,128,512]{3,2,1,0:T(8,128)(2,1)}, bf16[1,2,128,512]{3,2,1,0:T(8,128)(2,1)}, u32[]{:S(2)}, u32[]{:S(2)}) collective-permute-start(bf16[1,2,128,512]{3,2,1,0:T(8,128)(2,1)} %get-tuple-element.25), channel_id=1, source_target_pairs={{1,0},{3,2},{5,4},{7,6},{9,8},{11,10},{13,12},{15,14},{17,16},{19,... | collective-permute-start | bytes 786440 | tf_op jit(solution)/shard_map/ppermute | solution.py:15
  33.8 3.3 copy-start.26
  37.1 4.3 %copy-start.17 = (bf16[512,512]{1,0:T(8,128)(2,1)S(1)}, bf16[512,512]{1,0:T(8,128)(2,1)}, u32[]{:S(2)}) copy-start(bf16[512,512]{1,0:T(8,128)(2,1)} %param.19) | copy-start | bytes 1572868
  43.3 2.0 copy-start.14
  43.3 2.0 copy-start.25
  53.0 3.2 copy-start.7
  56.1 2.7 copy-start.3
  56.1 2.8 copy-start.4
  60.1 1.6 copy-start.27
  61.7 1.4 copy-start.16
  61.7 1.6 copy-start.23
  63.3 1.6 copy-start.6
  63.3 1.9 copy-start.13
  68.5 34.9 %sort.19.cloned.1.call-start = ((), (), s32[]{:S(2)}) async-start(), calls=%async_computation.2 | async-start | bytes 24608 | tf_op jit(solution)/shard_map/jit(argsort)/sort | solution.py:165
  69.8 278.8 %all-reduce.5.cloned.1.call-start = ((), (), s32[]{:S(2)}) async-start(), calls=%async_computation.1 | async-start | bytes 14680064 | tf_op jit(solution)/shard_map/psum | solution.py:197
  104.9 1.4 copy-start.8
  121.0 9.2 %copy-start.5 = (f32[768,512]{1,0:T(8,128)S(1)}, f32[768,512]{1,0:T(8,128)}, u32[]{:S(2)}) copy-start(f32[768,512]{1,0:T(8,128)} %get-tuple-element.13) | copy-start | bytes 4718596
  121.8 10.5 %collective-permute-start.4 = (bf16[1,2,128,512]{3,1,2,0:T(2,128)(2,1)S(1)}, bf16[1,2,128,512]{3,1,2,0:T(2,128)(2,1)S(1)}, u32[]{:S(2)}, u32[]{:S(2)}) collective-permute-start(bf16[1,2,128,512]{3,1,2,0:T(2,128)(2,1)S(1)} %get-tuple-element.15), channel_id=1, source_target_pairs={{0,2},{2,4},{4,6},{6,8},{8,10},{10,12},{12,14},{14,16},{16,18},{18... | collective-permute-start | bytes 786440 | tf_op jit(solution)/shard_map/ppermute | solution.py:12
  125.5 13.6 %collective-permute-start.5 = (bf16[1,2,128,512]{3,1,2,0:T(2,128)(2,1)S(1)}, bf16[1,2,128,512]{3,1,2,0:T(2,128)(2,1)S(1)}, u32[]{:S(2)}, u32[]{:S(2)}) collective-permute-start(bf16[1,2,128,512]{3,1,2,0:T(2,128)(2,1)S(1)} %get-tuple-element.18), channel_id=1, source_target_pairs={{2,0},{4,2},{6,4},{8,6},{10,8},{12,10},{14,12},{16,14},{18,16},{20... | collective-permute-start | bytes 786440 | tf_op jit(solution)/shard_map/ppermute | solution.py:15
  126.8 12.9 %collective-permute-start.6 = (bf16[1,2,128,512]{3,1,2,0:T(2,128)(2,1)S(1)}, bf16[1,2,128,512]{3,1,2,0:T(2,128)(2,1)S(1)}, u32[]{:S(2)}, u32[]{:S(2)}) collective-permute-start(bf16[1,2,128,512]{3,1,2,0:T(2,128)(2,1)S(1)} %get-tuple-element.17), channel_id=1, source_target_pairs={{0,1},{2,3},{4,5},{6,7},{8,9},{10,11},{12,13},{14,15},{16,17},{18,... | collective-permute-start | bytes 786440 | tf_op jit(solution)/shard_map/ppermute | solution.py:12
  128.7 11.0 %collective-permute-start.7 = (bf16[1,2,128,512]{3,1,2,0:T(2,128)(2,1)S(1)}, bf16[1,2,128,512]{3,1,2,0:T(2,128)(2,1)S(1)}, u32[]{:S(2)}, u32[]{:S(2)}) collective-permute-start(bf16[1,2,128,512]{3,1,2,0:T(2,128)(2,1)S(1)} %get-tuple-element.16), channel_id=1, source_target_pairs={{1,0},{3,2},{5,4},{7,6},{9,8},{11,10},{13,12},{15,14},{17,16},{19,... | collective-permute-start | bytes 786440 | tf_op jit(solution)/shard_map/ppermute | solution.py:15
  141.5 3.3 copy-start.12
  (7 other events, 7.7 us)
Sparse Core Ops, SparseCore 0:
  68.7 34.6 all-reduce.2
  109.4 239.1 all-reduce.4
Sparse Core Ops, SparseCore 1:
  71.8 2.2 sort.21.cloned.1.call-done
  (1 shorter events, 0.0 us)
